TPU v7x, 128 devices: a whole 4x4x4 slice. The times are simulated.
128 devices in a mesh: dp: 8 (over x_lo, y), expert: 16 (over x_hi, z, core).
Axes of the slice: x: 4 (x_hi: 2, x_lo: 2; x = x_hi * 2 + x_lo), y: 4, z: 4, core: 2. Of those that a mesh axis runs over, the one named last changes fastest.
Arguments:
- tokens: bfloat16 [65536, 2048], P(('dp', 'expert')), may hold values from -6 to 6
- probe: bfloat16 [65536, 2048], P(('dp', 'expert')), may hold values from -20 to 20
- domain: int32 [65536], P(('dp', 'expert')), may hold values from 0 to 21
- mix: float32 [22], replicated, may hold values from 0.5 to 2
- router: bfloat16 [2048, 32], replicated, may hold values from -0.125 to 0.125
- picks: int32 [128, 32, 40], P(('dp', 'expert')), may hold values from 0 to 511, as said below
- w_gate: bfloat16 [2048, 32, 768], P(None, 'expert'), may hold values from -0.125 to 0.125
- w_up: bfloat16 [2048, 32, 768], P(None, 'expert'), may hold values from -0.125 to 0.125
- w_down: bfloat16 [2048, 32, 768], P(None, 'expert'), may hold values from -0.21875 to 0.21875
Outputs:
- domain_loss: float32 [22], replicated
- router_grad: float32 [2048, 32], replicated
- grad_gate: bfloat16 [2048, 32, 768], P('dp', 'expert')
- grad_up: bfloat16 [2048, 32, 768], P('dp', 'expert')
- grad_down: bfloat16 [2048, 32, 768], P('dp', 'expert')
Inputs may be any that keep to these rules, and one draw needn't show every extreme that they name: The 40 picks of one expert on one device are distinct token positions of that device.
All inputs are finite; a program needn't handle non-finite values.
Results may differ from a plain program's by a relative error of at most 0.018.
Values may be sent and summed in bfloat16 or wider, within the bound.
A program may use at most 192 MiB of HBM per device.

v0:
```python
import math
import jax
import jax.numpy as jnp
from jax import lax
from jax.sharding import PartitionSpec as P

BF = jnp.bfloat16
F32 = jnp.float32


def body(tokens, probe, domain, mix, router, picks, w_gate, w_up, w_down):
    token_count, model_width = tokens.shape
    expert_count = router.shape[1]
    slot_count = picks.shape[2]
    pick_count = expert_count * slot_count
    domain_count = mix.shape[0]
    device_count = lax.axis_size("dp") * lax.axis_size("expert")
    flat = picks[0].reshape(pick_count)
    token_ids = jnp.arange(token_count, dtype=jnp.int32)
    select = (flat[:, None] == token_ids[None, :]).astype(BF)
    expert_of = jnp.repeat(jnp.arange(expert_count, dtype=jnp.int32), slot_count)
    own_expert = expert_of[:, None] == jnp.arange(expert_count, dtype=jnp.int32)[None, :]
    outgoing = jnp.dot(select, tokens, preferred_element_type=F32).astype(BF)
    received = lax.all_to_all(
        outgoing.reshape(expert_count, 1, slot_count, model_width),
        "expert",
        split_axis=0,
        concat_axis=1,
        tiled=True,
    )
    logits = jnp.dot(outgoing, router, preferred_element_type=F32)
    gate = jax.nn.sigmoid(jnp.sum(jnp.where(own_expert, logits, 0.0), axis=1))
    pre_gate = jnp.einsum("jsrd,djf->jsrf", received, w_gate, preferred_element_type=F32)
    pre_up = jnp.einsum("jsrd,djf->jsrf", received, w_up, preferred_element_type=F32)
    hidden = (jax.nn.silu(pre_gate) * pre_up).astype(BF)
    result = jnp.einsum("jsrf,djf->jsrd", hidden, w_down, preferred_element_type=F32).astype(BF)
    returned = lax.all_to_all(result, "expert", split_axis=1, concat_axis=0, tiled=True)
    returned = returned.reshape(pick_count, model_width)
    weighted = jnp.where(
        flat[None, :] == token_ids[:, None], gate.astype(BF)[None, :], jnp.zeros((), BF)
    )
    added = jnp.dot(weighted, returned, preferred_element_type=F32)
    difference = tokens.astype(F32) + added - probe.astype(F32)
    per_token = jnp.sum(difference * difference, axis=1)
    member = (domain[:, None] == jnp.arange(domain_count, dtype=jnp.int32)[None, :]).astype(F32)
    local_loss = jnp.sum(per_token[:, None] * member, axis=0)
    loss_scale = 1.0 / math.sqrt(device_count * slot_count)
    weight_tok = jnp.sum(member * mix[None, :], axis=1)
    upstream = ((loss_scale * weight_tok)[:, None] * difference).astype(BF)
    picked_up = jnp.dot(select, upstream, preferred_element_type=F32)
    sending = (gate[:, None] * picked_up).astype(BF)
    gate_slope = jnp.sum(picked_up * returned.astype(F32), axis=1)
    logit_grad = gate_slope * gate * (1.0 - gate)
    placing = jnp.where(own_expert, logit_grad[:, None], 0.0)
    high = placing.astype(BF)
    low = (placing - high.astype(F32)).astype(BF)
    placed = lax.dot_general(
        select,
        jnp.concatenate([high, low], axis=1),
        (((0,), (0,)), ((), ())),
        preferred_element_type=F32,
    ).astype(BF)
    router_part = lax.dot_general(
        tokens, placed, (((0,), (0,)), ((), ())), preferred_element_type=F32
    )
    router_part = router_part[:, :expert_count] + router_part[:, expert_count:]
    loss_rows = jnp.zeros((8, expert_count), F32).at[0, :domain_count].set(local_loss)
    summed = lax.psum(jnp.concatenate([router_part, loss_rows], axis=0), ("dp", "expert"))
    back_grad = lax.all_to_all(
        sending.reshape(expert_count, 1, slot_count, model_width),
        "expert",
        split_axis=0,
        concat_axis=1,
        tiled=True,
    )

    def reduced(left, right):
        part = jnp.einsum("jsrd,jsrf->djf", left, right, preferred_element_type=F32)
        return lax.psum_scatter(part.astype(BF), "dp", scatter_dimension=0, tiled=True)

    grad_down = reduced(back_grad, hidden)
    hidden_grad = jnp.einsum("jsrd,djf->jsrf", back_grad, w_down, preferred_element_type=F32)
    sigmoid_gate = jax.nn.sigmoid(pre_gate)
    gate_in = (
        hidden_grad * pre_up * sigmoid_gate * (1.0 + pre_gate * (1.0 - sigmoid_gate))
    ).astype(BF)
    up_in = (hidden_grad * (pre_gate * sigmoid_gate)).astype(BF)
    grad_gate = reduced(received, gate_in)
    grad_up = reduced(received, up_in)
    domain_loss = summed[model_width, :domain_count] * (
        domain_count / (token_count * device_count * model_width)
    )
    return (domain_loss, summed[:model_width], grad_gate, grad_up, grad_down)


def solution(mesh):
    placed = (
        P(("dp", "expert"), None),
        P(("dp", "expert"), None),
        P(("dp", "expert")),
        P(),
        P(),
        P(("dp", "expert"), None, None),
        P(None, "expert", None),
        P(None, "expert", None),
        P(None, "expert", None),
    )
    return jax.shard_map(
        body,
        mesh=mesh,
        in_specs=placed,
        out_specs=(
            P(),
            P(),
            P("dp", "expert", None),
            P("dp", "expert", None),
            P("dp", "expert", None),
        ),
        check_vma=False,
    )
```

profile of v0, /device:TPU:1, one launch (start us, length us, event | category | flops | bytes accessed | tf_op | source)
XLA Modules:
  0.0 530.8 jit_solution(12913081817586084446)
XLA Ops:
  8.9 4.9 convolution_convert_fusion
  13.8 71.2 %all_to_all.51 = bf16[32,1,40,2048]{3,2,1,0:T(8,128)(2,1)S(1)} all-to-all(bf16[32,1,40,2048]{3,2,1,0:T(8,128)(2,1)S(1)} %bitcast.69), channel_id=1, replica_groups=mesh['dp'=8,'expert'=16] {'expert'}, dimensions={0} | all-to-all | bytes 10485760 | tf_op jit(solution)/shard_map/all_to_all | solution.py:24
  85.0 4.4 fusion.5
  89.4 6.5 %multiply_convert_fusion.4 = (bf16[2,16,40,768]{3,2,1,0:T(8,128)(2,1)}, f32[2,16,40,768]{3,2,1,0:T(8,128)}) fusion(f32[2,16,40,768]{3,2,1,0:T(8,128)S(1)} %fusion.5, bf16[2048,2,768,1]{2,1,0,3:T(2,128)(2,1)S(1)} %bitcast.79, bf16[16,2,1,40,2048]{4,3,1,0,2:T(8,128)(2,1)S(1)} %bitcast.71), kind=kOutput, calls=%fused_computation.31 | convolution fusion | flops 4032430080 | bytes 21364736 | tf_op jit(solution)/shard_map/jsrd,djf->jsrf/dot_general | solution.py:34
  96.0 7.7 %fusion.19 = bf16[2,16,40,2048]{3,2,1,0:T(8,128)(2,1)S(1)} fusion(bf16[2,16,40,768]{3,2,1,0:T(8,128)(2,1)} %get-tuple-element.43, bf16[2048,2,768,1]{2,1,0,3:T(2,128)(2,1)} %bitcast.80), kind=kOutput, calls=%fused_computation.28 | convolution fusion | flops 4029153280 | bytes 13500416 | tf_op jit(solution)/shard_map/jsrf,djf->jsrd/dot_general | solution.py:36
  103.6 2.8 copy.51
  106.4 5.7 %all-to-all-start.1 = ((bf16[2,16,40,2048]{3,2,0,1:T(8,128)(2,1)}), bf16[2,16,40,2048]{3,2,0,1:T(8,128)(2,1)}, u32[]{:S(2)}, u32[]{:S(2)}) async-start(bf16[2,16,40,2048]{3,2,0,1:T(8,128)(2,1)} %copy.51), calls=%async_computation.1 | async-start | bytes 10485760 | tf_op jit(solution)/shard_map/all_to_all | solution.py:37
  112.2 4.3 fusion.38
  116.6 64.9 %all-to-all-done.1 = bf16[2,16,40,2048]{3,2,0,1:T(8,128)(2,1)} async-done(((bf16[2,16,40,2048]{3,2,0,1:T(8,128)(2,1)}), bf16[2,16,40,2048]{3,2,0,1:T(8,128)(2,1)}, u32[]{:S(2)}, u32[]{:S(2)}) %all-to-all-start.1) | async-done | bytes 5242912 | tf_op jit(solution)/shard_map/all_to_all | solution.py:37
  181.5 6.5 %multiply_reduce_fusion.1 = (f32[512]{0:T(512)S(1)}, f32[512,2048]{1,0:T(8,128)S(1)}) fusion(bf16[512,2048]{1,0:T(8,128)(2,1)} %param.12, bf16[1280,2048]{1,0:T(8,128)(2,1)} %bitcast.11, s32[1280]{0:T(1024)S(1)} %eq.64, bf16[1280]{0:T(1024)(128)(2,1)S(1)} %get-tuple-element.42, bf16[512,2048]{1,0:T(8,128)(2,1)S(1)} %copy-done.4), kind=kOutput, calls=%fused_computation.25 | convolution fusion | flops 2691956224 | bytes 13641216 | tf_op jit(solution)/shard_map/dot_general | solution.py:42
  188.1 7.4 %multiply_convert_fusion = (bf16[1280,2048]{1,0:T(8,128)(2,1)}, f32[1280]{0:T(1024)S(1)}) fusion(f32[1280]{0:T(1024)S(1)} %get-tuple-element.41, bf16[2,16,40,2048]{3,2,0,1:T(8,128)(2,1)} %all-to-all-done.1, f32[512,2048]{1,0:T(8,128)S(1)} %get-tuple-element.46, f32[512]{0:T(512)S(1)} %broadcast_multiply_fusion, s32[1280]{0:T(1024)S(1)} %eq.64), kind=kOutput, calls=%fused_computation.3 | convolution fusion | flops 2700212992 | bytes 14697472 | tf_op jit(solution)/shard_map/dot_general | solution.py:50
  195.5 14.7 %all-to-all-start.2 = ((bf16[32,1,40,2048]{3,2,1,0:T(8,128)(2,1)}), bf16[32,1,40,2048]{3,2,1,0:T(8,128)(2,1)}, u32[]{:S(2)}, u32[]{:S(2)}) async-start(bf16[32,1,40,2048]{3,2,1,0:T(8,128)(2,1)} %bitcast.74), calls=%async_computation.2 | async-start | bytes 10485760 | tf_op jit(solution)/shard_map/all_to_all | solution.py:69
  212.3 68.4 %all-to-all-done.2 = bf16[32,1,40,2048]{3,2,1,0:T(8,128)(2,1)} async-done(((bf16[32,1,40,2048]{3,2,1,0:T(8,128)(2,1)}), bf16[32,1,40,2048]{3,2,1,0:T(8,128)(2,1)}, u32[]{:S(2)}, u32[]{:S(2)}) %all-to-all-start.2) | async-done | bytes 5242912 | tf_op jit(solution)/shard_map/all_to_all | solution.py:69
  280.7 9.8 %fusion.2 = bf16[2048,2,768]{0,2,1:T(8,128)(2,1)} fusion(bf16[2,16,40,768]{3,2,1,0:T(8,128)(2,1)} %get-tuple-element.43, bf16[16,2,1,40,2048]{4,3,1,0,2:T(8,128)(2,1)} %bitcast.18), kind=kOutput, calls=%fused_computation.8 | convolution fusion | flops 4029677568 | bytes 13500416 | tf_op jit(solution)/shard_map/jsrd,jsrf->djf/dot_general | solution.py:78
  290.8 8.2 %fusion.7 = f32[2,16,40,768]{3,2,1,0:T(8,128)S(1)} fusion(bf16[2048,2,768,1]{2,1,0,3:T(2,128)(2,1)} %bitcast.81, bf16[16,2,1,40,2048]{4,3,1,0,2:T(8,128)(2,1)} %bitcast.18), kind=kOutput, calls=%fused_computation.13 | convolution fusion | flops 4026531840 | bytes 15466496 | tf_op jit(solution)/shard_map/jsrd,djf->jsrf/dot_general | solution.py:82
  299.0 1.8 copy-done.10
  300.9 9.9 %fusion.1 = bf16[2048,2,768]{0,2,1:T(8,128)(2,1)} fusion(bf16[16,2,1,40,2048]{4,3,1,0,2:T(8,128)(2,1)} %bitcast.72, f32[2,16,40,768]{3,2,1,0:T(8,128)S(1)} %fusion.7, f32[2,16,40,768]{3,2,1,0:T(8,128)S(1)} %copy-done.9), kind=kOutput, calls=%fused_computation.7 | convolution fusion | flops 4035575808 | bytes 19398656 | tf_op jit(solution)/shard_map/jsrd,jsrf->djf/dot_general | solution.py:78
  310.8 12.3 %fusion = bf16[2048,2,768]{0,2,1:T(8,128)(2,1)} fusion(bf16[16,2,1,40,2048]{4,3,1,0,2:T(8,128)(2,1)} %bitcast.73, f32[2,16,40,768]{3,2,1,0:T(8,128)} %copy-done.8, f32[2,16,40,768]{3,2,1,0:T(8,128)} %copy-done.10, f32[2,16,40,768]{3,2,1,0:T(8,128)} %get-tuple-element.44), kind=kOutput, calls=%fused_computation.6 | convolution fusion | flops 4039507968 | bytes 23330816 | tf_op jit(solution)/shard_map/jsrd,jsrf->djf/dot_general | solution.py:78
  323.2 129.6 %all-reduce.3.cloned.1.call-done = f32[2056,32]{0,1:T(8,128)} async-done(((f32[2056,32]{0,1:T(8,128)}), f32[2056,32]{0,1:T(8,128)}) %all-reduce.3.cloned.1.call-update) | async-done | bytes 263184 | tf_op jit(solution)/shard_map/psum | solution.py:68
  452.8 1.7 slice.35
  455.8 3.1 copy.58
  458.9 3.0 copy.57
  461.9 58.3 %reduce-scatter.4.cloned.1.call-done = bf16[256,2,768]{0,2,1:T(8,128)(2,1)} async-done(((bf16[2048,2,768]{0,2,1:T(8,128)(2,1)}), bf16[256,2,768]{0,2,1:T(8,128)(2,1)}) %reduce-scatter.4.cloned.1.call-update) | async-done | bytes 786448 | tf_op jit(solution)/shard_map/reduce_scatter | solution.py:79
  520.2 3.0 copy.56
  (50 shorter events, 4.9 us)
Async XLA Ops:
  8.0 104.2 %copy-start = (bf16[2048,32]{0,1:T(8,128)(2,1)S(1)}, bf16[2048,32]{0,1:T(8,128)(2,1)}, u32[]{:S(2)}) copy-start(bf16[2048,32]{0,1:T(8,128)(2,1)} %param.15) | copy-start | bytes 393220
  13.8 71.2 %copy-start.2 = (bf16[1280,2048]{1,0:T(8,128)(2,1)}, bf16[1280,2048]{1,0:T(8,128)(2,1)S(1)}, u32[]{:S(2)}) copy-start(bf16[1280,2048]{1,0:T(8,128)(2,1)S(1)} %convolution_convert_fusion) | copy-start | bytes 15728644
  13.8 71.2 %copy-start.7 = (bf16[2048,2,768]{2,1,0:T(2,128)(2,1)S(1)}, bf16[2048,2,768]{2,1,0:T(2,128)(2,1)}, u32[]{:S(2)}) copy-start(bf16[2048,2,768]{2,1,0:T(2,128)(2,1)} %param.17) | copy-start | bytes 18874372
  13.8 75.6 %slice-start = ((s8[6291456]{0:T(1024)(128)(4,1)}), s8[4194304]{0:T(1024)(128)(4,1)S(1)}, s32[]{:S(2)}) async-start(s8[6291456]{0:T(1024)(128)(4,1)} %bitcast.77), calls=%async_computation.10 | async-start | bytes 8388608
  85.0 4.4 copy-start.3
  85.0 4.4 slice-start.1
  89.4 6.6 %copy-start.8 = (f32[2,16,40,768]{3,2,1,0:T(8,128)}, f32[2,16,40,768]{3,2,1,0:T(8,128)S(1)}, u32[]{:S(2)}) copy-start(f32[2,16,40,768]{3,2,1,0:T(8,128)S(1)} %fusion.5) | copy-start | bytes 11796484
  106.4 75.0 %all-to-all-start.1 = ((bf16[2,16,40,2048]{3,2,0,1:T(8,128)(2,1)}), bf16[2,16,40,2048]{3,2,0,1:T(8,128)(2,1)}, u32[]{:S(2)}, u32[]{:S(2)}) async-start(bf16[2,16,40,2048]{3,2,0,1:T(8,128)(2,1)} %copy.51), calls=%async_computation.1 | async-start | bytes 10485760 | tf_op jit(solution)/shard_map/all_to_all | solution.py:37
  112.1 69.3 %copy-start.4 = (bf16[512,2048]{1,0:T(8,128)(2,1)S(1)}, bf16[512,2048]{1,0:T(8,128)(2,1)}, u32[]{:S(2)}) copy-start(bf16[512,2048]{1,0:T(8,128)(2,1)} %param.11) | copy-start | bytes 6291460
  181.5 6.5 %copy-start.5 = (s32[512]{0:T(512)S(1)}, s32[512]{0:T(512)}, u32[]{:S(2)}) copy-start(s32[512]{0:T(512)} %param.13) | copy-start | bytes 6148
  181.5 6.5 %copy-start.6 = (f32[22]{0:T(128)S(1)}, f32[22]{0:T(128)}, u32[]{:S(2)}) copy-start(f32[22]{0:T(128)} %param.14) | copy-start | bytes 268
  195.5 85.2 %all-to-all-start.2 = ((bf16[32,1,40,2048]{3,2,1,0:T(8,128)(2,1)}), bf16[32,1,40,2048]{3,2,1,0:T(8,128)(2,1)}, u32[]{:S(2)}, u32[]{:S(2)}) async-start(bf16[32,1,40,2048]{3,2,1,0:T(8,128)(2,1)} %bitcast.74), calls=%async_computation.2 | async-start | bytes 10485760 | tf_op jit(solution)/shard_map/all_to_all | solution.py:69
  210.2 242.6 %all-reduce.3.cloned.1.call-start = ((), (), s32[]{:S(2)}) async-start(), calls=%async_computation.6 | async-start | bytes 557056 | tf_op jit(solution)/shard_map/psum | solution.py:68
  212.2 243.5 %reduce-scatter.8.cloned.1.call-start = ((), (), s32[]{:S(2)}) async-start(), calls=%async_computation.9 | async-start | bytes 7077888 | tf_op jit(solution)/shard_map/reduce_scatter | solution.py:79
  290.5 168.3 %reduce-scatter.6.cloned.1.call-start = ((), (), s32[]{:S(2)}) async-start(), calls=%async_computation.8 | async-start | bytes 7077888 | tf_op jit(solution)/shard_map/reduce_scatter | solution.py:79
  290.8 10.1 %copy-start.9 = (f32[2,16,40,768]{3,2,1,0:T(8,128)S(1)}, f32[2,16,40,768]{3,2,1,0:T(8,128)}, u32[]{:S(2)}) copy-start(f32[2,16,40,768]{3,2,1,0:T(8,128)} %copy-done.8) | copy-start | bytes 11796484
  299.0 1.9 copy-start.10
  310.8 209.4 %reduce-scatter.4.cloned.1.call-start = ((), (), s32[]{:S(2)}) async-start(), calls=%async_computation.7 | async-start | bytes 7077888 | tf_op jit(solution)/shard_map/reduce_scatter | solution.py:79
  323.1 200.1 %copy-start.1 = (bf16[2048,32]{0,1:T(8,128)(2,1)S(1)}, bf16[2048,32]{0,1:T(8,128)(2,1)}, u32[]{:S(2)}) copy-start(bf16[2048,32]{0,1:T(8,128)(2,1)} %param.15) | copy-start | bytes 393220
Sparse Core Ops, SparseCore 0:
  216.3 236.3 all-reduce.2
Sparse Core Ops, SparseCore 1:
  290.6 81.2 reduce-scatter.7
  374.2 71.8 reduce-scatter.5
  448.3 71.9 reduce-scatter.3
where the time goes:
time: 531 us
  waiting for transfers between devices  321 us (60%)
  matrix products  82.8 us (16%)
  blocking collectives  71.2 us (13%)
  starting transfers between devices  20.8 us (4%)
  local copies, waits for them, and re-layouts  16.6 us (3%)
  between operations  15.9 us (3%)
    psum x1, waiting for transfers between devices, body(): lax.psum(jnp.concatenate([router_part, loss_rows], axis=0), ('dp', 'exper...  130 us
    all_to_all x1, blocking collectives, body(): lax.all_to_all(outgoing.reshape(expert_count, 1, slot_count, model_width)...  71.2 us
    all_to_all x1, waiting for transfers between devices, body(): lax.all_to_all(sending.reshape(expert_count, 1, slot_count, model_width),...  68.4 us
    all_to_all x1, waiting for transfers between devices, body(): lax.all_to_all(result, 'expert', split_axis=1, concat_axis=0, tiled=True)  64.9 us
    reduce_scatter x3, waiting for transfers between devices, reduced(): lax.psum_scatter(part.astype(BF), 'dp', scatter_dimension=0, tiled=True)  58.3 us
    dot_general x3, matrix products, reduced(): part = jnp.einsum('jsrd,jsrf->djf', left, right, preferred_element_type=F32)  32 us
    all_to_all x1, starting transfers between devices, body(): lax.all_to_all(sending.reshape(expert_count, 1, slot_count, model_width),...  14.7 us
    unnamed x29, local copies, waits for them, and re-layouts  11.1 us
  transfers between devices with their start and end apart: 6, of which 4 were waited for; matrix products, arithmetic and copies ran while one was open for 10% of the time, Pallas kernels for 0%

commit v1 on v0

--- a/solution.py
+++ b/solution.py
@@ -34,7 +34,10 @@
     pre_up = jnp.einsum("jsrd,djf->jsrf", received, w_up, preferred_element_type=F32)
     hidden = (jax.nn.silu(pre_gate) * pre_up).astype(BF)
     result = jnp.einsum("jsrf,djf->jsrd", hidden, w_down, preferred_element_type=F32).astype(BF)
-    returned = lax.all_to_all(result, "expert", split_axis=1, concat_axis=0, tiled=True)
+    size = lax.axis_size("expert")
+    tiles = jnp.stack(jnp.split(result, size, axis=1), axis=0)
+    tiles = lax.all_to_all(tiles, "expert", split_axis=0, concat_axis=0)
+    returned = jnp.concatenate(tiles, axis=0)
     returned = returned.reshape(pick_count, model_width)
     weighted = jnp.where(
         flat[None, :] == token_ids[:, None], gate.astype(BF)[None, :], jnp.zeros((), BF)

time: 531 us -> 541 us (1.019)
  local copies, waits for them, and re-layouts: 16.6 us -> 25.9 us
    unnamed x29 -> x44, local copies, waits for them, and re-layouts: 11.1 us -> 22.4 us
where the time goes in v1:
time: 541 us; the launch traced here: 540 us
  waiting for transfers between devices  321 us (59%)
  matrix products  82.8 us (15%)
  blocking collectives  71.2 us (13%)
  local copies, waits for them, and re-layouts  25.9 us (5%)
  starting transfers between devices  20.8 us (4%)
  between operations  15.9 us (3%)
    psum x1, waiting for transfers between devices, body(): lax.psum(jnp.concatenate([router_part, loss_rows], axis=0), ('dp', 'exper...  130 us
    all_to_all x1, blocking collectives, body(): lax.all_to_all(outgoing.reshape(expert_count, 1, slot_count, model_width)...  71.2 us
    all_to_all x1, waiting for transfers between devices, body(): lax.all_to_all(sending.reshape(expert_count, 1, slot_count, model_width),...  68.4 us
    all_to_all x1, waiting for transfers between devices, body(): tiles = lax.all_to_all(tiles, 'expert', split_axis=0, concat_axis=0)  64.9 us
    reduce_scatter x3, waiting for transfers between devices, reduced(): lax.psum_scatter(part.astype(BF), 'dp', scatter_dimension=0, tiled=True)  58.3 us
    dot_general x3, matrix products, reduced(): part = jnp.einsum('jsrd,jsrf->djf', left, right, preferred_element_type=F32)  32 us
    unnamed x44, local copies, waits for them, and re-layouts  22.4 us
    all_to_all x1, starting transfers between devices, body(): lax.all_to_all(sending.reshape(expert_count, 1, slot_count, model_width),...  14.7 us
  transfers between devices with their start and end apart: 6, of which 4 were waited for; matrix products, arithmetic and copies ran while one was open for 10% of the time, Pallas kernels for 0%

profile of v1, /device:TPU:1, one launch (start us, length us, event | category | flops | bytes accessed | tf_op | source)
XLA Modules:
  0.0 540.2 jit_solution(15996807720750897143)
XLA Ops:
  8.9 4.9 convolution_convert_fusion
  13.8 71.2 %all_to_all.41 = bf16[32,1,40,2048]{3,2,1,0:T(8,128)(2,1)S(1)} all-to-all(bf16[32,1,40,2048]{3,2,1,0:T(8,128)(2,1)S(1)} %bitcast.159), channel_id=1, replica_groups=mesh['dp'=8,'expert'=16] {'expert'}, dimensions={0} | all-to-all | bytes 10485760 | tf_op jit(solution)/shard_map/all_to_all | solution.py:24
  85.0 4.4 fusion.5
  89.4 6.5 %multiply_convert_fusion.4 = (bf16[2,16,40,768]{3,2,1,0:T(8,128)(2,1)}, f32[2,16,40,768]{3,2,1,0:T(8,128)}) fusion(f32[2,16,40,768]{3,2,1,0:T(8,128)S(1)} %fusion.5, bf16[2048,2,768,1]{2,1,0,3:T(2,128)(2,1)S(1)} %bitcast.169, bf16[16,2,1,40,2048]{4,3,1,0,2:T(8,128)(2,1)S(1)} %bitcast.161), kind=kOutput, calls=%fused_computation.31 | convolution fusion | flops 4032430080 | bytes 21364736 | tf_op jit(solution)/shard_map/jsrd,djf->jsrf/dot_general | solution.py:34
  96.0 7.7 %fusion.19 = bf16[2,16,40,2048]{3,2,1,0:T(8,128)(2,1)S(1)} fusion(bf16[2,16,40,768]{3,2,1,0:T(8,128)(2,1)} %get-tuple-element.43, bf16[2048,2,768,1]{2,1,0,3:T(2,128)(2,1)} %bitcast.170), kind=kOutput, calls=%fused_computation.28 | convolution fusion | flops 4029153280 | bytes 13500416 | tf_op jit(solution)/shard_map/jsrf,djf->jsrd/dot_general | solution.py:36
  115.8 5.7 %all-to-all-start.1 = ((bf16[16,2,1,40,2048]{4,3,1,2,0:T(8,128)(2,1)}), bf16[16,2,1,40,2048]{4,3,1,2,0:T(8,128)(2,1)}, u32[]{:S(2)}, u32[]{:S(2)}) async-start(bf16[16,2,1,40,2048]{4,3,1,2,0:T(8,128)(2,1)} %fusion.42), calls=%async_computation.1 | async-start | bytes 10485760 | tf_op jit(solution)/shard_map/all_to_all | solution.py:39
  121.6 4.3 fusion.38
  125.9 64.9 %all-to-all-done.1 = bf16[16,2,1,40,2048]{4,3,1,2,0:T(8,128)(2,1)} async-done(((bf16[16,2,1,40,2048]{4,3,1,2,0:T(8,128)(2,1)}), bf16[16,2,1,40,2048]{4,3,1,2,0:T(8,128)(2,1)}, u32[]{:S(2)}, u32[]{:S(2)}) %all-to-all-start.1) | async-done | bytes 5242912 | tf_op jit(solution)/shard_map/all_to_all | solution.py:39
  190.8 6.5 %multiply_reduce_fusion.1 = (f32[512]{0:T(512)S(1)}, f32[512,2048]{1,0:T(8,128)S(1)}) fusion(bf16[512,2048]{1,0:T(8,128)(2,1)} %param.12, bf16[1280,2048]{1,0:T(8,128)(2,1)} %bitcast.25, s32[1280]{0:T(1024)S(1)} %eq.64, bf16[1280]{0:T(1024)(128)(2,1)S(1)} %get-tuple-element.42, bf16[512,2048]{1,0:T(8,128)(2,1)S(1)} %copy-done.4), kind=kOutput, calls=%fused_computation.25 | convolution fusion | flops 2691956224 | bytes 13641216 | tf_op jit(solution)/shard_map/dot_general | solution.py:45
  197.4 7.4 %multiply_convert_fusion = (bf16[1280,2048]{1,0:T(8,128)(2,1)}, f32[1280]{0:T(1024)S(1)}) fusion(f32[1280]{0:T(1024)S(1)} %get-tuple-element.41, bf16[16,2,1,40,2048]{4,3,1,2,0:T(8,128)(2,1)} %all-to-all-done.1, f32[512,2048]{1,0:T(8,128)S(1)} %get-tuple-element.46, f32[512]{0:T(512)S(1)} %broadcast_multiply_fusion, s32[1280]{0:T(1024)S(1)} %eq.64), kind=kOutput, calls=%fused_computation.3 | convolution fusion | flops 2700212992 | bytes 14697472 | tf_op jit(solution)/shard_map/dot_general | solution.py:53
  204.8 14.7 %all-to-all-start.2 = ((bf16[32,1,40,2048]{3,2,1,0:T(8,128)(2,1)}), bf16[32,1,40,2048]{3,2,1,0:T(8,128)(2,1)}, u32[]{:S(2)}, u32[]{:S(2)}) async-start(bf16[32,1,40,2048]{3,2,1,0:T(8,128)(2,1)} %bitcast.164), calls=%async_computation.2 | async-start | bytes 10485760 | tf_op jit(solution)/shard_map/all_to_all | solution.py:72
  221.6 68.4 %all-to-all-done.2 = bf16[32,1,40,2048]{3,2,1,0:T(8,128)(2,1)} async-done(((bf16[32,1,40,2048]{3,2,1,0:T(8,128)(2,1)}), bf16[32,1,40,2048]{3,2,1,0:T(8,128)(2,1)}, u32[]{:S(2)}, u32[]{:S(2)}) %all-to-all-start.2) | async-done | bytes 5242912 | tf_op jit(solution)/shard_map/all_to_all | solution.py:72
  290.0 9.8 %fusion.2 = bf16[2048,2,768]{0,2,1:T(8,128)(2,1)} fusion(bf16[2,16,40,768]{3,2,1,0:T(8,128)(2,1)} %get-tuple-element.43, bf16[16,2,1,40,2048]{4,3,1,0,2:T(8,128)(2,1)} %bitcast.30), kind=kOutput, calls=%fused_computation.8 | convolution fusion | flops 4029677568 | bytes 13500416 | tf_op jit(solution)/shard_map/jsrd,jsrf->djf/dot_general | solution.py:81
  300.1 8.2 %fusion.7 = f32[2,16,40,768]{3,2,1,0:T(8,128)S(1)} fusion(bf16[2048,2,768,1]{2,1,0,3:T(2,128)(2,1)} %bitcast.171, bf16[16,2,1,40,2048]{4,3,1,0,2:T(8,128)(2,1)} %bitcast.30), kind=kOutput, calls=%fused_computation.13 | convolution fusion | flops 4026531840 | bytes 15466496 | tf_op jit(solution)/shard_map/jsrd,djf->jsrf/dot_general | solution.py:85
  308.3 1.8 copy-done.10
  310.2 9.9 %fusion.1 = bf16[2048,2,768]{0,2,1:T(8,128)(2,1)} fusion(bf16[16,2,1,40,2048]{4,3,1,0,2:T(8,128)(2,1)} %bitcast.162, f32[2,16,40,768]{3,2,1,0:T(8,128)S(1)} %fusion.7, f32[2,16,40,768]{3,2,1,0:T(8,128)S(1)} %copy-done.9), kind=kOutput, calls=%fused_computation.7 | convolution fusion | flops 4035575808 | bytes 19398656 | tf_op jit(solution)/shard_map/jsrd,jsrf->djf/dot_general | solution.py:81
  320.1 12.3 %fusion = bf16[2048,2,768]{0,2,1:T(8,128)(2,1)} fusion(bf16[16,2,1,40,2048]{4,3,1,0,2:T(8,128)(2,1)} %bitcast.163, f32[2,16,40,768]{3,2,1,0:T(8,128)} %copy-done.8, f32[2,16,40,768]{3,2,1,0:T(8,128)} %copy-done.10, f32[2,16,40,768]{3,2,1,0:T(8,128)} %get-tuple-element.44), kind=kOutput, calls=%fused_computation.6 | convolution fusion | flops 4039507968 | bytes 23330816 | tf_op jit(solution)/shard_map/jsrd,jsrf->djf/dot_general | solution.py:81
  332.5 129.6 %all-reduce.3.cloned.1.call-done = f32[2056,32]{0,1:T(8,128)} async-done(((f32[2056,32]{0,1:T(8,128)}), f32[2056,32]{0,1:T(8,128)}) %all-reduce.3.cloned.1.call-update) | async-done | bytes 263184 | tf_op jit(solution)/shard_map/psum | solution.py:71
  462.1 1.7 slice.35
  463.8 1.3 fusion.65
  465.1 3.1 copy.115
  468.2 3.0 copy.114
  471.2 58.3 %reduce-scatter.4.cloned.1.call-done = bf16[256,2,768]{0,2,1:T(8,128)(2,1)} async-done(((bf16[2048,2,768]{0,2,1:T(8,128)(2,1)}), bf16[256,2,768]{0,2,1:T(8,128)(2,1)}) %reduce-scatter.4.cloned.1.call-update) | async-done | bytes 786448 | tf_op jit(solution)/shard_map/reduce_scatter | solution.py:82
  529.5 3.0 copy.113
  (65 shorter events, 15.6 us)
Async XLA Ops:
  8.0 113.6 %copy-start = (bf16[2048,32]{0,1:T(8,128)(2,1)S(1)}, bf16[2048,32]{0,1:T(8,128)(2,1)}, u32[]{:S(2)}) copy-start(bf16[2048,32]{0,1:T(8,128)(2,1)} %param.15) | copy-start | bytes 393220
  13.8 71.2 %copy-start.2 = (bf16[1280,2048]{1,0:T(8,128)(2,1)}, bf16[1280,2048]{1,0:T(8,128)(2,1)S(1)}, u32[]{:S(2)}) copy-start(bf16[1280,2048]{1,0:T(8,128)(2,1)S(1)} %convolution_convert_fusion) | copy-start | bytes 15728644
  13.8 71.2 %copy-start.7 = (bf16[2048,2,768]{2,1,0:T(2,128)(2,1)S(1)}, bf16[2048,2,768]{2,1,0:T(2,128)(2,1)}, u32[]{:S(2)}) copy-start(bf16[2048,2,768]{2,1,0:T(2,128)(2,1)} %param.17) | copy-start | bytes 18874372
  13.8 75.6 %slice-start = ((s8[6291456]{0:T(1024)(128)(4,1)}), s8[4194304]{0:T(1024)(128)(4,1)S(1)}, s32[]{:S(2)}) async-start(s8[6291456]{0:T(1024)(128)(4,1)} %bitcast.167), calls=%async_computation.10 | async-start | bytes 8388608
  85.0 4.4 copy-start.3
  85.0 4.4 slice-start.1
  89.4 6.6 %copy-start.8 = (f32[2,16,40,768]{3,2,1,0:T(8,128)}, f32[2,16,40,768]{3,2,1,0:T(8,128)S(1)}, u32[]{:S(2)}) copy-start(f32[2,16,40,768]{3,2,1,0:T(8,128)S(1)} %fusion.5) | copy-start | bytes 11796484
  115.8 75.0 %all-to-all-start.1 = ((bf16[16,2,1,40,2048]{4,3,1,2,0:T(8,128)(2,1)}), bf16[16,2,1,40,2048]{4,3,1,2,0:T(8,128)(2,1)}, u32[]{:S(2)}, u32[]{:S(2)}) async-start(bf16[16,2,1,40,2048]{4,3,1,2,0:T(8,128)(2,1)} %fusion.42), calls=%async_computation.1 | async-start | bytes 10485760 | tf_op jit(solution)/shard_map/all_to_all | solution.py:39
  121.4 69.3 %copy-start.4 = (bf16[512,2048]{1,0:T(8,128)(2,1)S(1)}, bf16[512,2048]{1,0:T(8,128)(2,1)}, u32[]{:S(2)}) copy-start(bf16[512,2048]{1,0:T(8,128)(2,1)} %param.11) | copy-start | bytes 6291460
  190.8 6.5 %copy-start.5 = (s32[512]{0:T(512)S(1)}, s32[512]{0:T(512)}, u32[]{:S(2)}) copy-start(s32[512]{0:T(512)} %param.13) | copy-start | bytes 6148
  190.8 6.5 %copy-start.6 = (f32[22]{0:T(128)S(1)}, f32[22]{0:T(128)}, u32[]{:S(2)}) copy-start(f32[22]{0:T(128)} %param.14) | copy-start | bytes 268
  204.8 85.2 %all-to-all-start.2 = ((bf16[32,1,40,2048]{3,2,1,0:T(8,128)(2,1)}), bf16[32,1,40,2048]{3,2,1,0:T(8,128)(2,1)}, u32[]{:S(2)}, u32[]{:S(2)}) async-start(bf16[32,1,40,2048]{3,2,1,0:T(8,128)(2,1)} %bitcast.164), calls=%async_computation.2 | async-start | bytes 10485760 | tf_op jit(solution)/shard_map/all_to_all | solution.py:72
  219.5 242.6 %all-reduce.3.cloned.1.call-start = ((), (), s32[]{:S(2)}) async-start(), calls=%async_computation.6 | async-start | bytes 557056 | tf_op jit(solution)/shard_map/psum | solution.py:71
  221.5 243.5 %reduce-scatter.8.cloned.1.call-start = ((), (), s32[]{:S(2)}) async-start(), calls=%async_computation.9 | async-start | bytes 7077888 | tf_op jit(solution)/shard_map/reduce_scatter | solution.py:82
  299.9 168.3 %reduce-scatter.6.cloned.1.call-start = ((), (), s32[]{:S(2)}) async-start(), calls=%async_computation.8 | async-start | bytes 7077888 | tf_op jit(solution)/shard_map/reduce_scatter | solution.py:82
  300.1 10.1 %copy-start.9 = (f32[2,16,40,768]{3,2,1,0:T(8,128)S(1)}, f32[2,16,40,768]{3,2,1,0:T(8,128)}, u32[]{:S(2)}) copy-start(f32[2,16,40,768]{3,2,1,0:T(8,128)} %copy-done.8) | copy-start | bytes 11796484
  308.3 1.9 copy-start.10
  320.1 209.4 %reduce-scatter.4.cloned.1.call-start = ((), (), s32[]{:S(2)}) async-start(), calls=%async_computation.7 | async-start | bytes 7077888 | tf_op jit(solution)/shard_map/reduce_scatter | solution.py:82
  332.4 200.1 %copy-start.1 = (bf16[2048,32]{0,1:T(8,128)(2,1)S(1)}, bf16[2048,32]{0,1:T(8,128)(2,1)}, u32[]{:S(2)}) copy-start(bf16[2048,32]{0,1:T(8,128)(2,1)} %param.15) | copy-start | bytes 393220
Sparse Core Ops, SparseCore 0:
  225.7 236.3 all-reduce.2
Sparse Core Ops, SparseCore 1:
  299.9 81.2 reduce-scatter.7
  383.5 71.8 reduce-scatter.5
  457.6 71.9 reduce-scatter.3
